TPU v7x, 256 devices: a whole 4x4x8 slice. The times are simulated.
256 devices in a mesh: kmer: 16 (over y, z_hi), samp: 16 (over z_lo, x, core).
Axes of the slice: x: 4, y: 4, z: 8 (z_hi: 4, z_lo: 2; z = z_hi * 2 + z_lo), core: 2. Of those that a mesh axis runs over, the one named last changes fastest.
Arguments:
- tiles: bfloat16 [22528, 128, 128], P(('kmer', 'samp')), may hold values from 0 to 8
- omega: bfloat16 [16384, 128], P('samp'), may hold values from -0.5 to 0.5
- tile_rows: int32 [22528], P(('kmer', 'samp')), may hold values from 0 to 55, as said below
- tile_cols: int32 [22528], P(('kmer', 'samp')), may hold values from 0 to 7
- tile_count: int32 [256], P(('kmer', 'samp')), may hold values from 11 to 88, as said below
Outputs:
- sketch: bfloat16 [114688, 128], P(('kmer', 'samp'))
- co_sketch: float32 [16384, 128], P(('samp', 'kmer'))
Inputs may be any that keep to these rules, and one draw needn't show every extreme that they name: `tile_rows`: on each device the used slots name distinct pairs of k-mer block and sample block. `tile_count`: at least one device uses all 88 slots.
All inputs are finite; a program needn't handle non-finite values.
Results may differ from a plain program's by a relative error of at most 0.014.
Values may be sent and summed in bfloat16 or wider, within the bound.
No kernel may reach another device: no remote copies, remote signals or barrier semaphores. Data moves between devices by JAX's collectives and lax.ppermute only.
A program may use at most 64 MiB of HBM per device.

v0:
```python
import jax
import jax.numpy as jnp
from jax import lax
from jax.sharding import PartitionSpec as P

KB_DEV = 56


def forward_terms(tiles, table, tile_rows, tile_cols, count, out_blocks):
    slot_total = tiles.shape[0]
    live = lax.iota(jnp.int32, slot_total) < count
    chosen = table[tile_cols]
    prod = jnp.einsum("tkc,tcr->tkr", tiles, chosen, preferred_element_type=jnp.float32)
    prod = jnp.where(live[:, None, None], prod, jnp.float32(0.0))
    return jax.ops.segment_sum(prod, tile_rows, num_segments=out_blocks)


def backward_terms(tiles, table, tile_rows, tile_cols, count, out_blocks):
    slot_total = tiles.shape[0]
    live = lax.iota(jnp.int32, slot_total) < count
    picked = table[tile_rows]
    prod = jnp.einsum("tkc,tkr->tcr", tiles, picked, preferred_element_type=jnp.float32)
    prod = jnp.where(live[:, None, None], prod, jnp.float32(0.0))
    return jax.ops.segment_sum(prod, tile_cols, num_segments=out_blocks)


def shards(tiles, omega, tile_rows, tile_cols, tile_count):
    tile = tiles.shape[1]
    rank = omega.shape[1]
    sample_blocks = omega.shape[0] // tile
    count = tile_count[0]
    omega_blocks = omega.reshape(sample_blocks, tile, rank)
    partial_rows = forward_terms(tiles, omega_blocks, tile_rows, tile_cols, count, KB_DEV)
    partial_rows = partial_rows.reshape(KB_DEV * tile, rank)
    summed = lax.psum(partial_rows.astype(jnp.bfloat16), "samp")
    own_rows = summed.shape[0] // lax.axis_size("samp")
    sketch = lax.dynamic_slice_in_dim(summed, lax.axis_index("samp") * own_rows, own_rows, 0)
    sketch_blocks = summed.reshape(KB_DEV, tile, rank)
    co_partial = backward_terms(tiles, sketch_blocks, tile_rows, tile_cols, count, sample_blocks)
    co_partial = co_partial.reshape(sample_blocks * tile, rank)
    factor = 1.0 / (KB_DEV * tile * lax.axis_size("kmer")) ** 0.5
    co_total = lax.psum(co_partial.astype(jnp.bfloat16), "kmer").astype(jnp.float32)
    share_rows = co_total.shape[0] // lax.axis_size("kmer")
    co_sketch = lax.dynamic_slice_in_dim(
        co_total, lax.axis_index("kmer") * share_rows, share_rows, 0
    ) * jnp.float32(factor)
    return (sketch, co_sketch)


def solution(mesh):
    placed = (
        P(("kmer", "samp"), None, None),
        P("samp", None),
        P(("kmer", "samp")),
        P(("kmer", "samp")),
        P(("kmer", "samp")),
    )
    return jax.shard_map(
        shards,
        mesh=mesh,
        in_specs=placed,
        out_specs=(P(("kmer", "samp"), None), P(("samp", "kmer"), None)),
        check_vma=False,
    )
```

profile of v0, /device:TPU:2, one launch (start us, length us, event | category | flops | bytes accessed | tf_op | source)
XLA Modules:
  0.0 385.4 jit_solution(12764706739560385234)
XLA Ops:
  7.2 0.0 copy-start
  7.2 0.0 all-reduce.3.cloned.1.call-start
  8.0 0.7 compare_select_fusion.1
  8.7 3.6 gather_fusion
  12.3 0.0 copy-done
  12.3 6.6 %select_bitcast_fusion.1 = f32[88,128,128]{1,2,0:T(8,128)} fusion(pred[88]{0:T(512)(128)(4,1)S(1)} %iota_compare_fusion, bf16[88,128,128]{2,1,0:T(8,128)(2,1)} %gather_fusion, bf16[88,128,128]{2,1,0:T(8,128)(2,1)S(1)} %copy-done), kind=kOutput, calls=%fused_computation.5 | convolution fusion | flops 370540544 | bytes 11534424 | tf_op jit(solution)/shard_map/tkc,tcr->tkr/dot_general | solution.py:13
  18.9 6.3 %copy.10 = f32[88,128,128]{2,1,0:T(8,128)} copy(f32[88,128,128]{1,2,0:T(8,128)} %select_bitcast_fusion.1) | data formatting | bytes 11534336 | tf_op jit(solution)/shard_map/jit(_where)/select_n | solution.py:14
  25.1 0.0 copy-start.1
  25.1 2.3 broadcast_in_dim.36
  27.4 0.0 copy-done.1
  27.4 20.1 %scatter_fusion = f32[56,128,128]{2,1,0:T(8,128)} fusion(f32[56,128,128]{2,1,0:T(8,128)} %broadcast_in_dim.36, s32[88]{0:T(128)S(1)} %copy-done.1, f32[88,128,128]{2,1,0:T(8,128)} %copy.10), kind=kCustom, calls=%fused_computation.2 | custom fusion | flops 1441792 | bytes 17301856 | tf_op jit(solution)/shard_map/scatter-add | solution.py:15
  47.5 3.6 convert_element_type.15
  51.1 0.0 all-reduce.3.cloned.1.call-update
  51.1 0.0 all-reduce.5.cloned.1.call-start
  51.2 125.8 %all-reduce.3.cloned.1.call-done = bf16[7168,128]{1,0:T(8,128)(2,1)} async-done(((bf16[7168,128]{1,0:T(8,128)(2,1)}), bf16[7168,128]{1,0:T(8,128)(2,1)}) %all-reduce.3.cloned.1.call-update) | async-done | bytes 1835024 | tf_op jit(solution)/shard_map/psum | solution.py:35
  176.9 4.1 %gather_fusion.1 = bf16[88,128,128]{2,1,0:T(8,128)(2,1)} fusion(bf16[56,128,128]{2,1,0:T(8,128)(2,1)} %bitcast.16, s32[1024]{0:T(1024)S(1)} %pad_clamp_fusion), kind=kCustom, calls=%fused_computation.1 | custom fusion | bytes 5767520 | tf_op jit(solution)/shard_map/gather | solution.py:21
  181.0 5.7 %select_bitcast_fusion = f32[88,128,128]{1,2,0:T(8,128)} fusion(pred[88]{0:T(512)(128)(4,1)S(1)} %iota_compare_fusion, bf16[88,128,128]{2,1,0:T(8,128)(2,1)} %gather_fusion.1, bf16[88,128,128]{2,1,0:T(8,128)(2,1)S(1)} %copy-done), kind=kOutput, calls=%fused_computation.4 | convolution fusion | flops 370540544 | bytes 11534424 | tf_op jit(solution)/shard_map/tkc,tkr->tcr/dot_general | solution.py:22
  186.7 0.0 copy-start.2
  186.7 6.3 %copy.12 = f32[88,128,128]{2,1,0:T(8,128)} copy(f32[88,128,128]{1,2,0:T(8,128)} %select_bitcast_fusion) | data formatting | bytes 11534336 | tf_op jit(solution)/shard_map/jit(_where)/select_n | solution.py:23
  193.1 0.0 copy-done.2
  193.1 12.7 %scatter_fusion.1 = f32[8,128,128]{2,1,0:T(8,128)S(1)} fusion(f32[8,128,128]{2,1,0:T(8,128)S(1)} %broadcast_in_dim.41, s32[88]{0:T(128)S(1)} %copy-done.2, f32[88,128,128]{2,1,0:T(8,128)} %copy.12), kind=kCustom, calls=%fused_computation.3 | custom fusion | flops 1441792 | bytes 17301856 | tf_op jit(solution)/shard_map/scatter-add | solution.py:24
  205.8 0.7 convert_element_type.17
  206.6 0.0 all-reduce.5.cloned.1.call-update
  206.6 1.6 constant_dynamic-slice_fusion
  208.2 169.1 %all-reduce.5.cloned.1.call-done = bf16[1024,128]{1,0:T(8,128)(2,1)} async-done(((bf16[1024,128]{1,0:T(8,128)(2,1)}), bf16[1024,128]{1,0:T(8,128)(2,1)}) %all-reduce.5.cloned.1.call-update) | async-done | bytes 262160 | tf_op jit(solution)/shard_map/psum | solution.py:42
  377.2 1.3 convert_multiply_fusion
  (5 shorter events, 0.1 us)
Async XLA Ops:
  7.2 5.1 %copy-start = (bf16[88,128,128]{2,1,0:T(8,128)(2,1)S(1)}, bf16[88,128,128]{2,1,0:T(8,128)(2,1)}, u32[]{:S(2)}) copy-start(bf16[88,128,128]{2,1,0:T(8,128)(2,1)} %param.5) | copy-start | bytes 8650756
  7.2 169.7 %all-reduce.3.cloned.1.call-start = ((), (), s32[]{:S(2)}) async-start(), calls=%async_computation | async-start | bytes 3670016 | tf_op jit(solution)/shard_map/psum | solution.py:35
  25.1 2.3 copy-start.1
  51.1 326.2 %all-reduce.5.cloned.1.call-start = ((), (), s32[]{:S(2)}) async-start(), calls=%async_computation.1 | async-start | bytes 524288 | tf_op jit(solution)/shard_map/psum | solution.py:42
  186.7 6.4 %copy-start.2 = (s32[88]{0:T(128)S(1)}, s32[88]{0:T(128)}, u32[]{:S(2)}) copy-start(s32[88]{0:T(128)} %param.8) | copy-start | bytes 1060
Sparse Core Ops, SparseCore 0:
  51.2 125.6 all-reduce.2
  206.7 170.4 all-reduce.4
where the time goes:
time: 386 us; the launch traced here: 385 us
  waiting for transfers between devices  295 us (76%)
  other arithmetic  39.1 us (10%)
  local copies, waits for them, and re-layouts  24.2 us (6%)
  between operations  14.9 us (4%)
  matrix products  12.3 us (3%)
    psum x1, waiting for transfers between devices, shards(): lax.psum(co_partial.astype(jnp.bfloat16), 'kmer').astype(jnp.float32)  169 us
    psum x1, waiting for transfers between devices, shards(): summed = lax.psum(partial_rows.astype(jnp.bfloat16), 'samp')  126 us
    scatter-add x1, other arithmetic, forward_terms(): return jax.ops.segment_sum(prod, tile_rows, num_segments=out_blocks)  20.1 us
    scatter-add x1, other arithmetic, backward_terms(): return jax.ops.segment_sum(prod, tile_cols, num_segments=out_blocks)  12.7 us
  transfers between devices with their start and end apart: 2, of which 2 were waited for; matrix products, arithmetic and copies ran while one was open for 0% of the time, Pallas kernels for 0%

commit v1 on v0

--- a/solution.py
+++ b/solution.py
@@ -32,7 +32,7 @@
     omega_blocks = omega.reshape(sample_blocks, tile, rank)
     partial_rows = forward_terms(tiles, omega_blocks, tile_rows, tile_cols, count, KB_DEV)
     partial_rows = partial_rows.reshape(KB_DEV * tile, rank)
-    summed = lax.psum(partial_rows.astype(jnp.bfloat16), "samp")
+    summed = jnp.sum(lax.all_gather(partial_rows.astype(jnp.bfloat16), "samp"), axis=0)
     own_rows = summed.shape[0] // lax.axis_size("samp")
     sketch = lax.dynamic_slice_in_dim(summed, lax.axis_index("samp") * own_rows, own_rows, 0)
     sketch_blocks = summed.reshape(KB_DEV, tile, rank)

time: 386 us -> 425 us (1.10)
  waiting for transfers between devices: 295 us -> 322 us
  other arithmetic: 39.1 us -> 50.8 us
    all_gather x0 -> x1, waiting for transfers between devices: none -> 156 us  [shards(): lax.all_gather(partial_rows.astype(jnp.bfloat16), 'samp')]
    psum x1 -> x0, waiting for transfers between devices: 126 us -> none  [shards(): summed = lax.psum(partial_rows.astype(jnp.bfloat16), 'samp')]
    reduce_sum x0 -> x1, other arithmetic: none -> 11.7 us  [shards(): jnp.sum(lax.all_gather(partial_rows.astype(jnp.bfloat16), 'samp'), axis=0)]
where the time goes in v1:
time: 425 us; the launch traced here: 424 us
  waiting for transfers between devices  322 us (76%)
  other arithmetic  50.8 us (12%)
  local copies, waits for them, and re-layouts  24.2 us (6%)
  between operations  14.9 us (4%)
  matrix products  12.3 us (3%)
    psum x1, waiting for transfers between devices, shards(): lax.psum(co_partial.astype(jnp.bfloat16), 'kmer').astype(jnp.float32)  166 us
    all_gather x1, waiting for transfers between devices, shards(): lax.all_gather(partial_rows.astype(jnp.bfloat16), 'samp')  156 us
    scatter-add x1, other arithmetic, forward_terms(): return jax.ops.segment_sum(prod, tile_rows, num_segments=out_blocks)  20.1 us
    scatter-add x1, other arithmetic, backward_terms(): return jax.ops.segment_sum(prod, tile_cols, num_segments=out_blocks)  12.7 us
    reduce_sum x1, other arithmetic, shards(): jnp.sum(lax.all_gather(partial_rows.astype(jnp.bfloat16), 'samp'), axis=0)  11.7 us
  transfers between devices with their start and end apart: 2, of which 2 were waited for; matrix products, arithmetic and copies ran while one was open for 0% of the time, Pallas kernels for 0%

profile of v1, /device:TPU:2, one launch (start us, length us, event | category | flops | bytes accessed | tf_op | source)
XLA Modules:
  0.0 423.8 jit_solution(11025390549979594727)
XLA Ops:
  7.2 0.0 copy-start
  7.2 0.0 all-gather.2.cloned.1.call-start
  8.0 0.7 compare_select_fusion.1
  8.7 3.6 gather_fusion
  12.3 0.0 copy-done
  12.3 6.6 %select_bitcast_fusion.1 = f32[88,128,128]{1,2,0:T(8,128)} fusion(pred[88]{0:T(512)(128)(4,1)S(1)} %iota_compare_fusion, bf16[88,128,128]{2,1,0:T(8,128)(2,1)} %gather_fusion, bf16[88,128,128]{2,1,0:T(8,128)(2,1)S(1)} %copy-done), kind=kOutput, calls=%fused_computation.5 | convolution fusion | flops 370540544 | bytes 11534424 | tf_op jit(solution)/shard_map/tkc,tcr->tkr/dot_general | solution.py:13
  18.9 6.3 %copy.14 = f32[88,128,128]{2,1,0:T(8,128)} copy(f32[88,128,128]{1,2,0:T(8,128)} %select_bitcast_fusion.1) | data formatting | bytes 11534336 | tf_op jit(solution)/shard_map/jit(_where)/select_n | solution.py:14
  25.1 0.0 copy-start.1
  25.1 2.3 broadcast_in_dim.36
  27.4 0.0 copy-done.1
  27.4 20.1 %scatter_fusion = f32[56,128,128]{2,1,0:T(8,128)} fusion(f32[56,128,128]{2,1,0:T(8,128)} %broadcast_in_dim.36, s32[88]{0:T(128)S(1)} %copy-done.1, f32[88,128,128]{2,1,0:T(8,128)} %copy.14), kind=kCustom, calls=%fused_computation.2 | custom fusion | flops 1441792 | bytes 17301856 | tf_op jit(solution)/shard_map/scatter-add | solution.py:15
  47.5 3.6 convert_element_type.24
  51.1 0.0 all-gather.2.cloned.1.call-update
  51.1 0.0 all-reduce.2.cloned.1.call-start
  51.2 155.9 %all-gather.2.cloned.1.call-done = bf16[16,7168,128]{2,1,0:T(8,128)(2,1)} async-done(((bf16[1,7168,128]{2,1,0:T(8,128)(2,1)}), bf16[16,7168,128]{2,1,0:T(8,128)(2,1)}) %all-gather.2.cloned.1.call-update) | async-done | bytes 29360144 | tf_op jit(solution)/shard_map/all_gather | solution.py:35
  207.1 11.7 %reduce_sum.12 = bf16[7168,128]{1,0:T(8,128)(2,1)} reduce(bf16[16,7168,128]{2,1,0:T(8,128)(2,1)} %all-gather.2.cloned.1.call-done, bf16[]{:T(256)} %constant.5.clone.1), dimensions={0}, to_apply=%region_1.2 | reduce | flops 13762560 | bytes 31195138 | tf_op jit(solution)/shard_map/reduce_sum | solution.py:35
  218.7 4.1 gather_fusion.1
  222.8 5.7 %select_bitcast_fusion = f32[88,128,128]{1,2,0:T(8,128)} fusion(pred[88]{0:T(512)(128)(4,1)S(1)} %iota_compare_fusion, bf16[88,128,128]{2,1,0:T(8,128)(2,1)} %gather_fusion.1, bf16[88,128,128]{2,1,0:T(8,128)(2,1)S(1)} %copy-done), kind=kOutput, calls=%fused_computation.4 | convolution fusion | flops 370540544 | bytes 11534424 | tf_op jit(solution)/shard_map/tkc,tkr->tcr/dot_general | solution.py:22
  228.6 0.0 copy-start.2
  228.6 6.3 %copy.16 = f32[88,128,128]{2,1,0:T(8,128)} copy(f32[88,128,128]{1,2,0:T(8,128)} %select_bitcast_fusion) | data formatting | bytes 11534336 | tf_op jit(solution)/shard_map/jit(_where)/select_n | solution.py:23
  234.9 0.0 copy-done.2
  234.9 12.7 %scatter_fusion.1 = f32[8,128,128]{2,1,0:T(8,128)S(1)} fusion(f32[8,128,128]{2,1,0:T(8,128)S(1)} %broadcast_in_dim.41, s32[88]{0:T(128)S(1)} %copy-done.2, f32[88,128,128]{2,1,0:T(8,128)} %copy.16), kind=kCustom, calls=%fused_computation.3 | custom fusion | flops 1441792 | bytes 17301856 | tf_op jit(solution)/shard_map/scatter-add | solution.py:24
  247.6 0.7 convert_element_type.26
  248.4 0.0 all-reduce.2.cloned.1.call-update
  248.4 1.6 constant_dynamic-slice_fusion
  250.0 165.7 %all-reduce.2.cloned.1.call-done = bf16[1024,128]{1,0:T(8,128)(2,1)} async-done(((bf16[1024,128]{1,0:T(8,128)(2,1)}), bf16[1024,128]{1,0:T(8,128)(2,1)}) %all-reduce.2.cloned.1.call-update) | async-done | bytes 262160 | tf_op jit(solution)/shard_map/psum | solution.py:42
  415.6 1.3 convert_multiply_fusion
  (5 shorter events, 0.1 us)
Async XLA Ops:
  7.2 5.1 %copy-start = (bf16[88,128,128]{2,1,0:T(8,128)(2,1)S(1)}, bf16[88,128,128]{2,1,0:T(8,128)(2,1)}, u32[]{:S(2)}) copy-start(bf16[88,128,128]{2,1,0:T(8,128)(2,1)} %param.5) | copy-start | bytes 8650756
  7.2 199.9 %all-gather.2.cloned.1.call-start = ((), (), s32[]{:S(2)}) async-start(), calls=%async_computation | async-start | bytes 31195136 | tf_op jit(solution)/shard_map/all_gather | solution.py:35
  25.1 2.3 copy-start.1
  51.1 364.5 %all-reduce.2.cloned.1.call-start = ((), (), s32[]{:S(2)}) async-start(), calls=%async_computation.1 | async-start | bytes 524288 | tf_op jit(solution)/shard_map/psum | solution.py:42
  228.6 6.4 %copy-start.2 = (s32[88]{0:T(128)S(1)}, s32[88]{0:T(128)}, u32[]{:S(2)}) copy-start(s32[88]{0:T(128)} %param.8) | copy-start | bytes 1060
Sparse Core Ops, SparseCore 0:
  51.2 155.7 all-gather.1
  248.5 167.0 all-reduce.1
